TPU v7x, 32 devices: a whole 2x2x4 slice. The times are simulated.
32 devices in a mesh: seq: 8 (over y, x, core), mp: 4 (over z).
Axes of the slice: x: 2, y: 2, z: 4, core: 2. Of those that a mesh axis runs over, the one named last changes fastest.
Arguments:
- tokens: bfloat16 [64, 2048, 1024], P('mp', 'seq'), may hold values from -6 to 6
- cotangent: bfloat16 [64, 2048, 1024], P('mp', 'seq'), may hold values from -6 to 6
- lengths: int32 [64], P('mp'), may hold values from 256 to 2048, as said below
- routed: int32 [64, 256], P('mp', 'seq'), may hold values from 0 to 2047, as said below
- gain_attn: float32 [1024], replicated, may hold values from 0.5 to 1.5
- gain_mlp: float32 [1024], replicated, may hold values from 0.5 to 1.5
- router: float32 [1024], replicated, may hold values from -0.1875 to 0.1875
- w_qkv: bfloat16 [3, 1024, 1024], P(None, None, 'mp'), may hold values from -0.1875 to 0.1875
- w_out: bfloat16 [1024, 1024], P('mp'), may hold values from -1.5 to 1.5
- w_mlp: bfloat16 [4096, 2, 1024], P('mp'), may hold values from -0.1875 to 0.1875
Outputs:
- layer_out: bfloat16 [64, 2048, 1024], P('mp', 'seq')
- grad_tokens: bfloat16 [64, 2048, 1024], P('mp', 'seq')
- grad_gain_attn: float32 [1024], replicated
- grad_gain_mlp: float32 [1024], replicated
- grad_router: float32 [1024], replicated
- grad_qkv: float32 [3, 1024, 1024], P(None, None, 'mp')
- grad_out: float32 [1024, 1024], P('mp')
- grad_mlp: float32 [4096, 2, 1024], P('mp')
Inputs may be any that keep to these rules, and one draw needn't show every extreme that they name: `lengths`: multiples of 8; of the two sequences 2 i and 2 i + 1 (aligned pairs) at most one is longer than 1024; among the 16 sequences of each index of mp one has length 2048 and its partner in the pair has length 256. `routed`: entry j of a sequence lies in 8 j to 8 j + 7; entries with j at or past lengths / 8 point at padding.
All inputs are finite; a program needn't handle non-finite values.
Results may differ from a plain program's by a relative error of at most 0.017.
Values may be sent and summed in bfloat16 or wider, within the bound.
No kernel may reach another device: no remote copies, remote signals or barrier semaphores. Data moves between devices by JAX's collectives and lax.ppermute only.
A program may use at most 192 MiB of HBM per device.

v0:
```python
import jax
import jax.numpy as jnp
from jax import lax
from jax.sharding import PartitionSpec as P

HEAD = 64
EPSILON = 1e-06
NEGATIVE = -1e30
BEST = lax.Precision.HIGHEST
CONTRACT_ROWS = (((0,), (0,)), ((), ()))
CONTRACT_COLS = (((1,), (1,)), ((), ()))


def rms_scale(values):
    return lax.rsqrt(jnp.mean(values * values, axis=-1, keepdims=True) + EPSILON)


def norm_back(grad_normed, unit_rows, scale, gain):
    scaled = gain * grad_normed
    return scale * (scaled - unit_rows * jnp.mean(unit_rows * scaled, axis=-1, keepdims=True))


def gelu_tanh(values):
    return jax.nn.gelu(values, approximate=True)


def split_heads(heads_in, unit_rows):
    local_width = heads_in.shape[2]
    batches = heads_in.shape[1] // unit_rows
    shaped = heads_in.reshape(3, batches, unit_rows, local_width // HEAD, HEAD)
    return (shaped[0], shaped[1], shaped[2])


def masked_scores(query, keys, split_row):
    raw = jnp.einsum("sqhd,skhd->shqk", query, keys, preferred_element_type=jnp.float32) * HEAD ** (
        -0.5
    )
    row_pos = lax.broadcasted_iota(jnp.int32, raw.shape, 2)
    col_pos = lax.broadcasted_iota(jnp.int32, raw.shape, 3)
    same = (row_pos >= split_row) == (col_pos >= split_row)
    return jnp.where(same & (row_pos >= col_pos), raw, NEGATIVE)


def holder_pass(held_rows, gain_attn, gain_mlp, router, w_qkv, w_out, w_mlp, unit_rows, split_row):
    held_float = held_rows.astype(jnp.float32)
    scale_one = rms_scale(held_float)
    unit_one = held_float * scale_one
    normed_one = (unit_one * gain_attn).astype(jnp.bfloat16)
    gate = jax.nn.sigmoid(jnp.dot(held_float, router, precision=BEST))
    normed_all = lax.all_gather(normed_one, "mp", axis=0, tiled=True)
    heads_in = jnp.einsum(
        "rd,cde->cre", normed_all, w_qkv, preferred_element_type=jnp.float32
    ).astype(jnp.bfloat16)
    query, keys, values = split_heads(heads_in, unit_rows)
    scores = masked_scores(query, keys, split_row)
    peak = jnp.max(scores, axis=-1, keepdims=True)
    raised = jnp.exp(scores - peak)
    totals = jnp.sum(raised, axis=-1, keepdims=True)
    weights = (raised / totals).astype(jnp.bfloat16)
    log_total = peak + jnp.log(totals)
    mixed = jnp.einsum(
        "shqk,skhd->sqhd", weights, values, preferred_element_type=jnp.float32
    ).astype(jnp.bfloat16)
    mixed = mixed.reshape(normed_all.shape[0], heads_in.shape[2])
    attended = lax.psum_scatter(
        jnp.dot(mixed, w_out, preferred_element_type=jnp.float32),
        "mp",
        scatter_dimension=0,
        tiled=True,
    )
    middle = held_float + attended
    scale_two = rms_scale(middle)
    unit_two = middle * scale_two
    normed_two = (unit_two * gain_mlp).astype(jnp.bfloat16)
    normed_mid = lax.all_gather(normed_two, "mp", axis=0, tiled=True)
    upward = lax.dot_general(
        normed_mid, w_mlp[:, 0, :], CONTRACT_COLS, preferred_element_type=jnp.float32
    )
    active = gelu_tanh(upward).astype(jnp.bfloat16)
    feed = lax.psum_scatter(
        jnp.dot(active, w_mlp[:, 1, :], preferred_element_type=jnp.float32).astype(jnp.bfloat16),
        "mp",
        scatter_dimension=0,
        tiled=True,
    ).astype(jnp.float32)
    return (
        held_float,
        scale_one,
        unit_one,
        gate,
        normed_all,
        heads_in,
        log_total,
        mixed,
        attended,
        scale_two,
        unit_two,
        normed_mid,
        upward,
        active,
        attended + feed,
        w_mlp,
    )


def on_device(tokens, cotangent, lengths, routed, gain_attn, gain_mlp, router, w_qkv, w_out, w_mlp):
    group, span, width = tokens.shape
    slots = routed.shape[1]
    ranks = lax.axis_size("seq")
    held = group // ranks
    seq_rows = slots * ranks
    rows = held * seq_rows
    inner = routed % 8
    place = lax.axis_index("seq") * slots + lax.broadcasted_iota(jnp.int32, routed.shape, 1)
    live = place < (lengths // 8)[:, None]
    token_grid = tokens.reshape(group, slots, 8, width)
    grad_grid = cotangent.reshape(group, slots, 8, width)
    pick = lax.broadcasted_iota(jnp.int32, (group, slots, 8), 2) == inner[:, :, None]
    chosen = jnp.take_along_axis(token_grid, inner[:, :, None, None], axis=2)
    chosen_grad = jnp.take_along_axis(grad_grid, inner[:, :, None, None], axis=2)
    chosen_grad = jnp.where(live[:, :, None, None], chosen_grad, jnp.zeros_like(chosen_grad))
    got_tokens, got_grads = (
        lax.all_to_all(
            chosen.reshape(ranks, held, 1, slots, width),
            "seq",
            split_axis=0,
            concat_axis=2,
            tiled=True,
        ),
        lax.all_to_all(
            chosen_grad.reshape(ranks, held, 1, slots, width),
            "seq",
            split_axis=0,
            concat_axis=2,
            tiled=True,
        ),
    )
    held_rows = got_tokens.reshape(rows, width)
    held_grads = got_grads.reshape(rows, width)
    first_pass = holder_pass(
        held_rows, gain_attn, gain_mlp, router, w_qkv, w_out, w_mlp, seq_rows, seq_rows
    )
    returned = (first_pass[3][:, None] * first_pass[14]).astype(jnp.bfloat16)
    saved = holder_pass(
        held_rows, gain_attn, gain_mlp, router, w_qkv, w_out, w_mlp, seq_rows, seq_rows
    )
    (
        held_float,
        scale_one,
        unit_one,
        gate,
        normed_all,
        heads_in,
        log_total,
        mixed,
        attended,
        scale_two,
        unit_two,
        normed_mid,
        upward,
        active,
        delta,
        full_mlp,
    ) = saved
    grad_rows = held_grads.astype(jnp.float32)
    grad_logit = jnp.sum(grad_rows * delta, axis=-1) * gate * (1.0 - gate)
    router_part = jnp.dot(grad_logit, held_float, precision=BEST)
    grad_feed = (gate[:, None] * grad_rows).astype(jnp.bfloat16)
    feed_all = lax.all_gather(grad_feed, "mp", axis=0, tiled=True)
    grad_active = lax.dot_general(
        feed_all, w_mlp[:, 1, :], CONTRACT_COLS, preferred_element_type=jnp.float32
    )
    unused, gelu_pull = jax.vjp(gelu_tanh, upward)
    grad_upward = gelu_pull(grad_active)[0].astype(jnp.bfloat16)
    up_part = lax.dot_general(
        grad_upward, normed_mid, CONTRACT_ROWS, preferred_element_type=jnp.float32
    )
    down_part = lax.dot_general(active, feed_all, CONTRACT_ROWS, preferred_element_type=jnp.float32)
    mlp_local = jnp.stack([up_part, down_part], axis=1)
    grad_normed_two = lax.psum_scatter(
        jnp.dot(grad_upward, w_mlp[:, 0, :], preferred_element_type=jnp.float32),
        "mp",
        scatter_dimension=0,
        tiled=True,
    )
    grad_middle = norm_back(grad_normed_two, unit_two, scale_two, gain_mlp)
    mlp_gain_part = jnp.sum(grad_normed_two * unit_two, axis=0)
    grad_attended = (gate[:, None] * grad_rows + grad_middle).astype(jnp.bfloat16)
    attended_all = lax.all_gather(grad_attended, "mp", axis=0, tiled=True)
    out_local = lax.dot_general(
        mixed, attended_all, CONTRACT_ROWS, preferred_element_type=jnp.float32
    )
    grad_mixed = lax.dot_general(
        attended_all, w_out, CONTRACT_COLS, preferred_element_type=jnp.float32
    ).astype(jnp.bfloat16)
    query, keys, values = split_heads(heads_in, seq_rows)
    grad_heads_mixed = grad_mixed.reshape(query.shape)
    scores = masked_scores(query, keys, seq_rows)
    shares = jnp.exp(scores - log_total)
    weights = shares.astype(jnp.bfloat16)
    grad_weights = jnp.einsum(
        "sqhd,skhd->shqk", grad_heads_mixed, values, preferred_element_type=jnp.float32
    )
    grad_scores = (
        shares * (grad_weights - jnp.sum(shares * grad_weights, axis=-1, keepdims=True))
    ).astype(jnp.bfloat16)
    grad_query = jnp.einsum(
        "shqk,skhd->sqhd", grad_scores, keys, preferred_element_type=jnp.float32
    ) * HEAD ** (-0.5)
    grad_keys = jnp.einsum(
        "shqk,sqhd->skhd", grad_scores, query, preferred_element_type=jnp.float32
    ) * HEAD ** (-0.5)
    grad_values = jnp.einsum(
        "shqk,sqhd->skhd", weights, grad_heads_mixed, preferred_element_type=jnp.float32
    )
    grad_heads = (
        jnp.stack([grad_query, grad_keys, grad_values]).astype(jnp.bfloat16).reshape(heads_in.shape)
    )
    qkv_local = jnp.einsum(
        "rd,cre->cde", normed_all, grad_heads, preferred_element_type=jnp.float32
    )
    grad_normed_one = lax.psum_scatter(
        jnp.einsum("cre,cde->rd", grad_heads, w_qkv, preferred_element_type=jnp.float32).astype(
            jnp.bfloat16
        ),
        "mp",
        scatter_dimension=0,
        tiled=True,
    ).astype(jnp.float32)
    attn_gain_part = jnp.sum(grad_normed_one * unit_one, axis=0)
    grad_picked = (
        grad_middle
        + norm_back(grad_normed_one, unit_one, scale_one, gain_attn)
        + grad_logit[:, None] * router
    ).astype(jnp.bfloat16)
    back_out, back_grad = (
        lax.all_to_all(
            returned.reshape(1, held, ranks, slots, width),
            "seq",
            split_axis=2,
            concat_axis=0,
            tiled=True,
        ),
        lax.all_to_all(
            grad_picked.reshape(1, held, ranks, slots, width),
            "seq",
            split_axis=2,
            concat_axis=0,
            tiled=True,
        ),
    )
    keep = pick[:, :, :, None] & live[:, :, None, None]
    back_out = back_out.reshape(group, slots, 1, width).astype(jnp.float32)
    back_grad = back_grad.reshape(group, slots, 1, width).astype(jnp.float32)
    layer_out = (token_grid.astype(jnp.float32) + jnp.where(keep, back_out, 0.0)).astype(
        jnp.bfloat16
    )
    grad_tokens = (grad_grid.astype(jnp.float32) + jnp.where(keep, back_grad, 0.0)).astype(
        jnp.bfloat16
    )
    grad_qkv, grad_out, grad_mlp = (
        lax.psum(qkv_local.astype(jnp.bfloat16), "seq").astype(jnp.float32),
        lax.psum(out_local.astype(jnp.bfloat16), "seq").astype(jnp.float32),
        lax.psum(mlp_local.astype(jnp.bfloat16), "seq").astype(jnp.float32),
    )
    grad_gain_attn, grad_gain_mlp, grad_router = lax.psum(
        (attn_gain_part, mlp_gain_part, router_part), ("seq", "mp")
    )
    return (
        layer_out.reshape(group, span, width),
        grad_tokens.reshape(group, span, width),
        grad_gain_attn,
        grad_gain_mlp,
        grad_router,
        grad_qkv,
        grad_out,
        grad_mlp,
    )


def solution(mesh):
    placed = (
        P("mp", "seq", None),
        P("mp", "seq", None),
        P("mp"),
        P("mp", "seq"),
        P(),
        P(),
        P(),
        P(None, None, "mp"),
        P("mp", None),
        P("mp", None, None),
    )
    return jax.shard_map(
        on_device,
        mesh=mesh,
        in_specs=placed,
        out_specs=(
            P("mp", "seq", None),
            P("mp", "seq", None),
            P(),
            P(),
            P(),
            P(None, None, "mp"),
            P("mp", None),
            P("mp", None, None),
        ),
        check_vma=False,
    )
```

profile of v0, /device:TPU:0, one launch (start us, length us, event | category | flops | bytes accessed | tf_op | source)
XLA Modules:
  0.0 1143.7 jit_solution(17167783072121866484)
XLA Ops:
  9.4 8.4 gather_fusion.1
  17.9 8.4 gather_fusion
  26.4 2.8 select_select_fusion
  29.2 20.3 %all_to_all.42 = bf16[8,2,1,32,1024]{4,3,1,2,0:T(8,128)(2,1)S(1)} all-to-all(bf16[8,2,1,32,1024]{4,3,1,2,0:T(8,128)(2,1)S(1)} %bitcast.192), channel_id=1, replica_groups=mesh['seq'=8,'mp'=4] {'seq'}, dimensions={0} | all-to-all | bytes 2097152 | tf_op jit(solution)/shard_map/all_to_all | solution.py:123
  53.2 80.2 %all-gather.5.cloned.1.call-done = bf16[2048,1024]{1,0:T(8,128)(2,1)} async-done(((bf16[512,1024]{1,0:T(8,128)(2,1)}), bf16[2048,1024]{1,0:T(8,128)(2,1)}) %all-gather.5.cloned.1.call-update) | async-done | bytes 4194320 | tf_op jit(solution)/shard_map/all_gather | solution.py:50
  133.4 5.6 fusion.25
  140.8 4.6 reshape.258
  145.4 3.9 copy.157
  149.3 4.4 reshape.257
  153.7 4.0 copy.156
  157.7 4.4 reshape.256
  162.1 4.0 copy.158
  166.0 3.9 fusion.71
  176.8 4.7 fusion.73
  181.6 143.1 %reduce-scatter.5.cloned.1.call-done = f32[512,1024]{1,0:T(8,128)} async-done(((f32[2048,1024]{1,0:T(8,128)}), f32[512,1024]{1,0:T(8,128)}) %reduce-scatter.5.cloned.1.call-update) | async-done | bytes 2097168 | tf_op jit(solution)/shard_map/reduce_scatter | solution.py:65
  324.7 2.1 multiply_reduce_fusion.3
  328.4 19.2 %all_to_all.43 = bf16[8,2,1,32,1024]{4,3,1,2,0:T(8,128)(2,1)S(1)} all-to-all(bf16[8,2,1,32,1024]{4,3,1,2,0:T(8,128)(2,1)} %bitcast.191), channel_id=1, replica_groups=mesh['seq'=8,'mp'=4] {'seq'}, dimensions={0} | all-to-all | bytes 2097152 | tf_op jit(solution)/shard_map/all_to_all | solution.py:130
  350.7 10.2 fusion.69
  360.9 49.1 %all-gather.7.cloned.1.call-done = bf16[2048,1024]{1,0:T(8,128)(2,1)} async-done(((bf16[512,1024]{1,0:T(8,128)(2,1)}), bf16[2048,1024]{1,0:T(8,128)(2,1)}) %all-gather.7.cloned.1.call-update) | async-done | bytes 4194320 | tf_op jit(solution)/shard_map/all_gather | solution.py:75
  410.0 10.3 fusion.58
  420.3 3.4 copy-done.36
  423.7 7.2 convolution_convert_fusion
  431.0 60.3 %all-gather.9.cloned.1.call-done = bf16[2048,1024]{1,0:T(8,128)(2,1)} async-done(((bf16[512,1024]{1,0:T(8,128)(2,1)}), bf16[2048,1024]{1,0:T(8,128)(2,1)}) %all-gather.9.cloned.1.call-update) | async-done | bytes 4194320 | tf_op jit(solution)/shard_map/all_gather | solution.py:169
  491.3 14.6 %fusion.10 = bf16[2048,1024]{1,0:T(8,128)(2,1)S(1)} fusion(f32[2048,1024]{1,0:T(8,128)} %copy-done.36, bf16[2048,1024]{1,0:T(8,128)(2,1)} %all-gather.9.cloned.1.call-done, bf16[1024,1,1024]{2,1,0:T(2,128)(2,1)} %get-tuple-element.63), kind=kOutput, calls=%fused_computation.16 | convolution fusion | flops 4336910336 | bytes 18874368 | tf_op jit(solution)/shard_map/dot_general | solution.py:170
  505.9 1.9 copy-done.35
  507.9 6.9 fusion.57
  514.8 54.0 %reduce-scatter.7.cloned.1.call-done = bf16[512,1024]{1,0:T(8,128)(2,1)} async-done(((bf16[2048,1024]{1,0:T(8,128)(2,1)}), bf16[512,1024]{1,0:T(8,128)(2,1)}) %reduce-scatter.7.cloned.1.call-update) | async-done | bytes 1048592 | tf_op jit(solution)/shard_map/reduce_scatter | solution.py:80
  568.8 147.9 %reduce-scatter.9.cloned.1.call-done = f32[512,1024]{1,0:T(8,128)} async-done(((f32[2048,1024]{1,0:T(8,128)}), f32[512,1024]{1,0:T(8,128)}) %reduce-scatter.9.cloned.1.call-update) | async-done | bytes 2097168 | tf_op jit(solution)/shard_map/reduce_scatter | solution.py:180
  716.7 5.3 multiply_reduce_fusion.1
  722.1 1.8 add_convert_fusion
  723.9 81.6 %all-gather.11.cloned.1.call-done = bf16[2048,1024]{1,0:T(8,128)(2,1)} async-done(((bf16[512,1024]{1,0:T(8,128)(2,1)}), bf16[2048,1024]{1,0:T(8,128)(2,1)}) %all-gather.11.cloned.1.call-update) | async-done | bytes 4194320 | tf_op jit(solution)/shard_map/all_gather | solution.py:189
  805.5 4.5 convolution_convert_fusion.1
  810.0 4.6 reshape.259
  814.5 3.9 copy.168
  818.5 6.3 fusion.52
  824.7 5.6 multiply_reduce_fusion
  830.4 2.0 multiply_convert_fusion
  832.4 2.4 fusion.56
  834.8 1.8 fusion.55
  836.6 4.0 copy.194
  840.6 4.3 reshape.255
  844.9 4.0 copy.192
  848.9 4.3 reshape.253
  853.3 4.0 copy.193
  857.3 4.3 reshape.254
  866.1 5.1 bitcast_convert_fusion
  871.4 8.2 convert_bitcast_fusion.2
  879.6 9.0 convert_bitcast_fusion.1
  888.6 2.5 pad_maximum_fusion
  892.6 2.1 convolution_convert_fusion.2
  896.0 4.5 fusion.44
  900.5 2.3 copy.163
  902.8 4.5 all-to-all-start.1
  907.3 39.2 %reduce-scatter.11.cloned.1.call-done = bf16[512,1024]{1,0:T(8,128)(2,1)} async-done(((bf16[2048,1024]{1,0:T(8,128)(2,1)}), bf16[512,1024]{1,0:T(8,128)(2,1)}) %reduce-scatter.11.cloned.1.call-update) | async-done | bytes 1048592 | tf_op jit(solution)/shard_map/reduce_scatter | solution.py:222
  946.6 2.0 fusion.38
  948.6 3.2 fusion.35
  953.0 4.2 all-to-all-start.3
  958.2 2.8 bitcast_convert_fusion.2
  961.1 106.0 %all-reduce.4.cloned.1.call-done = (bf16[3,1024,256]{1,2,0:T(8,128)(2,1)}, bf16[1024,2,1024]{2,0,1:T(8,128)(2,1)}, bf16[256,1024]{1,0:T(8,128)(2,1)}) async-done(((bf16[3,1024,256]{1,2,0:T(8,128)(2,1)}, bf16[1024,2,1024]{2,0,1:T(8,128)(2,1)}, bf16[256,1024]{1,0:T(8,128)(2,1)}), (bf16[3,1024,256]{1,2,0:T(8,128)(2,1)}, bf16[1024,2,1024]{2,0,1:T(8,128)(2,1)}, ...) | async-done | bytes 6291472 | tf_op jit(solution)/shard_map/psum | solution.py:262
  1067.0 2.1 convert_element_type.200
  1069.2 3.1 copy.185
  1072.2 9.9 copy.186
  1082.1 39.6 %all-reduce = (f32[1024]{0:T(1024)}, f32[1024]{0:T(1024)}, f32[1024]{0:T(1024)}) all-reduce(f32[1024]{0:T(1024)S(1)} %get-tuple-element.51, f32[1024]{0:T(1024)S(1)} %get-tuple-element.49, f32[1024]{0:T(1024)S(1)} %bitcast.204), channel_id=1, replica_groups=mesh['seq'=8,'mp'=4] {'seq','mp'}, use_global_device_ids=true, to_apply=%region_13.15 | all-reduce | flops 3072 | bytes 24576 | tf_op jit(solution)/shard_map/psum | solution.py:266
  1123.6 13.1 %fusion.1 = (bf16[16,256,1024]{2,1,0:T(8,128)(2,1)}, bf16[16,256,1024]{2,1,0:T(8,128)(2,1)}) fusion(bf16[16,256,1024]{2,1,0:T(8,128)(2,1)} %param.13, f32[16,32,1024]{2,1,0:T(8,128)S(1)} %bitcast.185, pred[16,256]{1,0:T(8,128)(4,1)S(1)} %copy.149, f32[16,32,1024]{2,1,0:T(8,128)S(1)} %bitcast.184, bf16[16,256,1024]{2,1,0:T(8,128)(2,1)} %param.12), kind=kLoop, calls=%fused_computation.4 | loop fusion | flops 33554432 | bytes 37752832 | tf_op jit(solution)/shard_map/convert_element_type | solution.py:258
  (141 shorter events, 30.8 us)
Async XLA Ops:
  7.2 126.3 %copy-start = (bf16[3,1024,256]{2,1,0:T(8,128)(2,1)S(1)}, bf16[3,1024,256]{2,1,0:T(8,128)(2,1)}, u32[]{:S(2)}) copy-start(bf16[3,1024,256]{2,1,0:T(8,128)(2,1)} %param.19) | copy-start | bytes 4718596
  7.2 126.2 %all-gather.5.cloned.1.call-start = ((), (), s32[]{:S(2)}) async-start(), calls=%async_computation.8 | async-start | bytes 5242880 | tf_op jit(solution)/shard_map/all_gather | solution.py:50
  8.7 0.6 copy-start.22
  26.4 2.8 copy-start.29
  26.4 25.4 %copy-start.25 = (f32[1024]{0:T(1024)S(1)}, f32[1024]{0:T(1024)}, u32[]{:S(2)}) copy-start(f32[1024]{0:T(1024)} %param.16) | copy-start | bytes 12292
  49.5 1.0 copy-start.8
  50.5 88.6 %copy-start.27 = (f32[512]{0:T(512)}, f32[512]{0:T(512)S(1)}, u32[]{:S(2)}) copy-start(f32[512]{0:T(512)S(1)} %rsqrt.22) | copy-start | bytes 6148
  53.1 271.6 %reduce-scatter.5.cloned.1.call-start = ((), (), s32[]{:S(2)}) async-start(), calls=%async_computation.9 | async-start | bytes 10485760 | tf_op jit(solution)/shard_map/reduce_scatter | solution.py:65
  169.9 3.4 copy-start.1
  169.9 3.4 copy-start.13
  174.9 1.9 copy-start.19
  175.8 1.0 copy-start.11
  181.5 145.3 %copy-start.24 = (f32[1024]{0:T(1024)S(1)}, f32[1024]{0:T(1024)}, u32[]{:S(2)}) copy-start(f32[1024]{0:T(1024)} %param.17) | copy-start | bytes 12292
  181.6 228.4 %all-gather.7.cloned.1.call-start = ((), (), s32[]{:S(2)}) async-start(), calls=%async_computation.10 | async-start | bytes 5242880 | tf_op jit(solution)/shard_map/all_gather | solution.py:75
  324.7 2.2 copy-start.2
  328.3 163.0 %all-gather.9.cloned.1.call-start = ((), (), s32[]{:S(2)}) async-start(), calls=%async_computation.12 | async-start | bytes 5242880 | tf_op jit(solution)/shard_map/all_gather | solution.py:169
  347.6 0.7 copy-start.31
  348.1 1.3 copy-start.4
  350.6 218.2 %reduce-scatter.7.cloned.1.call-start = ((), (), s32[]{:S(2)}) async-start(), calls=%async_computation.11 | async-start | bytes 5242880 | tf_op jit(solution)/shard_map/reduce_scatter | solution.py:80
  410.0 13.7 %copy-start.18 = (bf16[1024,1,1024]{2,1,0:T(2,128)(2,1)S(1)}, bf16[1024,1,1024]{2,1,0:T(2,128)(2,1)}, u32[]{:S(2)}) copy-start(bf16[1024,1,1024]{2,1,0:T(2,128)(2,1)} %get-tuple-element.63) | copy-start | bytes 6291460
  420.3 3.4 copy-start.36
  430.9 285.8 %reduce-scatter.9.cloned.1.call-start = ((), (), s32[]{:S(2)}) async-start(), calls=%async_computation.13 | async-start | bytes 10485760 | tf_op jit(solution)/shard_map/reduce_scatter | solution.py:180
  491.3 16.5 %copy-start.17 = (bf16[1024,1,1024]{2,1,0:T(2,128)(2,1)S(1)}, bf16[1024,1,1024]{2,1,0:T(2,128)(2,1)}, u32[]{:S(2)}) copy-start(bf16[1024,1,1024]{2,1,0:T(2,128)(2,1)} %get-tuple-element.62) | copy-start | bytes 6291460
  505.9 1.9 copy-start.35
  514.8 290.7 %all-gather.11.cloned.1.call-start = ((), (), s32[]{:S(2)}) async-start(), calls=%async_computation.14 | async-start | bytes 5242880 | tf_op jit(solution)/shard_map/all_gather | solution.py:189
  716.7 5.3 copy-start.3
  716.7 5.3 copy-start.5
  716.7 5.3 copy-start.6
  723.9 222.7 %reduce-scatter.11.cloned.1.call-start = ((), (), s32[]{:S(2)}) async-start(), calls=%async_computation.15 | async-start | bytes 5242880 | tf_op jit(solution)/shard_map/reduce_scatter | solution.py:222
  818.5 6.3 copy-start.7
  818.5 6.3 copy-start.14
  818.5 11.9 %slice-start = ((s8[8388608]{0:T(1024)(128)(4,1)}), s8[4194304]{0:T(1024)(128)(4,1)S(1)}, s32[]{:S(2)}) async-start(s8[8388608]{0:T(1024)(128)(4,1)} %bitcast.177), calls=%async_computation.17 | async-start | bytes 8388608
  824.7 5.6 slice-start.1
  830.4 2.0 copy-start.16
  832.4 2.4 copy-start.10
  861.6 2.7 copy-start.15
  864.4 1.7 copy-start.20
  871.1 195.9 %all-reduce.4.cloned.1.call-start = ((), (), s32[]{:S(2)}) async-start(), calls=%async_computation.16 | async-start | bytes 12582912 | tf_op jit(solution)/shard_map/psum | solution.py:262
  871.4 8.2 copy-start.33
  888.6 2.5 copy-start.12
  888.6 4.0 copy-start.34
  892.6 2.1 copy-start.21
  892.6 3.3 copy-start.32
  900.5 46.1 %copy-start.26 = (f32[1024]{0:T(1024)S(1)}, f32[1024]{0:T(1024)}, u32[]{:S(2)}) copy-start(f32[1024]{0:T(1024)} %param.16) | copy-start | bytes 12292
  900.5 46.1 %copy-start.28 = (f32[512]{0:T(512)S(1)}, f32[512]{0:T(512)}, u32[]{:S(2)}) copy-start(f32[512]{0:T(512)} %copy-done.27) | copy-start | bytes 6148
  902.8 50.2 %all-to-all-start.1 = ((bf16[1,2,8,32,1024]{4,3,1,0,2:T(8,128)(2,1)}), bf16[1,2,8,32,1024]{4,3,1,0,2:T(8,128)(2,1)}, u32[]{:S(2)}, u32[]{:S(2)}) async-start(bf16[1,2,8,32,1024]{4,3,1,0,2:T(8,128)(2,1)} %copy.163), calls=%async_computation.3 | async-start | bytes 2097152 | tf_op jit(solution)/shard_map/all_to_all | solution.py:237
  948.6 8.6 copy-start.30
  948.6 8.7 copy-start.23
  953.0 168.7 %all-to-all-start.3 = ((bf16[1,2,8,32,1024]{4,3,1,0,2:T(8,128)(2,1)}), bf16[1,2,8,32,1024]{4,3,1,0,2:T(8,128)(2,1)}, u32[]{:S(2)}, u32[]{:S(2)}) async-start(bf16[1,2,8,32,1024]{4,3,1,0,2:T(8,128)(2,1)} %copy.182), calls=%async_computation.7 | async-start | bytes 2097152 | tf_op jit(solution)/shard_map/all_to_all | solution.py:244
  1121.7 1.9 copy-start.9
Sparse Core Ops, SparseCore 0:
  53.3 80.1 all-gather.4
  181.7 143.0 reduce-scatter.4
  328.5 81.4 all-gather.6
  412.0 79.2 all-gather.8
  493.4 75.3 reduce-scatter.6
  571.7 144.9 reduce-scatter.8
  724.0 81.4 all-gather.10
  871.3 75.2 reduce-scatter.10
  950.7 116.3 all-reduce.3
where the time goes:
time: 1150 us; the launch traced here: 1140 us
  waiting for transfers between devices  762 us (66%)
  local copies, waits for them, and re-layouts  124 us (11%)
  matrix products  106 us (9%)
  blocking collectives  79.1 us (7%)
  other arithmetic  49.2 us (4%)
  between operations  14.8 us (1%)
    reduce_scatter x1, waiting for transfers between devices, on_device(): lax.psum_scatter(jnp.dot(grad_upward, w_mlp[:, 0, :], preferred_element_t...  148 us
    reduce_scatter x1, waiting for transfers between devices, holder_pass(): lax.psum_scatter(jnp.dot(mixed, w_out, preferred_element_type=jnp.float32...  143 us
    psum x1, waiting for transfers between devices, on_device(): lax.psum(qkv_local.astype(jnp.bfloat16), 'seq').astype(jnp.float32)  106 us
    all_gather x1, waiting for transfers between devices, on_device(): attended_all = lax.all_gather(grad_attended, 'mp', axis=0, tiled=True)  81.6 us
    all_gather x1, waiting for transfers between devices, holder_pass(): normed_all = lax.all_gather(normed_one, 'mp', axis=0, tiled=True)  80.2 us
    all_gather x1, waiting for transfers between devices, on_device(): feed_all = lax.all_gather(grad_feed, 'mp', axis=0, tiled=True)  60.3 us
    reduce_scatter x1, waiting for transfers between devices, holder_pass(): lax.psum_scatter(jnp.dot(active, w_mlp[:, 1, :], preferred_element_type=j...  54 us
    all_gather x1, waiting for transfers between devices, holder_pass(): normed_mid = lax.all_gather(normed_two, 'mp', axis=0, tiled=True)  49.1 us
  transfers between devices with their start and end apart: 11, of which 9 were waited for; matrix products, arithmetic and copies ran while one was open for 9% of the time, Pallas kernels for 0%

commit v1 on v0

--- a/solution.py
+++ b/solution.py
@@ -104,6 +104,27 @@
 
 
 def on_device(tokens, cotangent, lengths, routed, gain_attn, gain_mlp, router, w_qkv, w_out, w_mlp):
+
+    def make_the_outputs(my_tile, axis_id, out_dim):
+        f_now, mixed_arr, p_next = (
+            lax.axis_size(axis_id),
+            lax.axis_index(axis_id),
+            my_tile.shape[out_dim],
+        )
+        in_order = list(map(lambda dev: (dev, (dev + 1) % f_now), range(f_now)))
+        local_next = jnp.zeros(
+            (*my_tile.shape[:out_dim], f_now * p_next, *my_tile.shape[out_dim + 1 :]), my_tile.dtype
+        )
+        block_next = my_tile
+        for s in [*range(f_now)]:
+            carry_in = (mixed_arr - s) % f_now
+            local_next = lax.dynamic_update_slice_in_dim(
+                local_next, block_next, carry_in * p_next, axis=out_dim
+            )
+            if s < f_now - 1:
+                block_next = lax.ppermute(block_next, axis_id, in_order)
+        return local_next
+
     group, span, width = tokens.shape
     slots = routed.shape[1]
     ranks = lax.axis_size("seq")
@@ -166,7 +187,7 @@
     grad_logit = jnp.sum(grad_rows * delta, axis=-1) * gate * (1.0 - gate)
     router_part = jnp.dot(grad_logit, held_float, precision=BEST)
     grad_feed = (gate[:, None] * grad_rows).astype(jnp.bfloat16)
-    feed_all = lax.all_gather(grad_feed, "mp", axis=0, tiled=True)
+    feed_all = make_the_outputs(grad_feed, "mp", 0)
     grad_active = lax.dot_general(
         feed_all, w_mlp[:, 1, :], CONTRACT_COLS, preferred_element_type=jnp.float32
     )

time: 1150 us -> 1180 us (1.026)
  starting transfers between devices: 9.33 us -> 33.4 us
  blocking collectives: 79.1 us -> 59.9 us
  waiting for transfers between devices: 762 us -> 776 us
    ppermute x0 -> x3, waiting for transfers between devices: none -> 95.4 us  [make_the_outputs(): block_next = lax.ppermute(block_next, axis_id, in_order)]
    all_gather x1 -> x0, waiting for transfers between devices: 60.3 us -> none  [on_device(): feed_all = lax.all_gather(grad_feed, 'mp', axis=0, tiled=True)]
    reduce_scatter x1, waiting for transfers between devices: 54 us -> 0.02 us  [holder_pass(): lax.psum_scatter(jnp.dot(active, w_mlp[:, 1, :], preferred_element_type=j...]
    all_gather x1, waiting for transfers between devices: 49.1 us -> 71.2 us  [holder_pass(): normed_mid = lax.all_gather(normed_two, 'mp', axis=0, tiled=True)]
    ppermute x0 -> x3, starting transfers between devices: none -> 19.9 us  [make_the_outputs(): block_next = lax.ppermute(block_next, axis_id, in_order)]
    all_to_all x1 -> x0, blocking collectives: 19.2 us -> none  [on_device(): lax.all_to_all(chosen_grad.reshape(ranks, held, 1, slots, width), 'seq',...]
    all_to_all x0 -> x1, waiting for transfers between devices: none -> 15.3 us  [on_device(): lax.all_to_all(chosen_grad.reshape(ranks, held, 1, slots, width), 'seq',...]
    unnamed x83 -> x89, local copies, waits for them, and re-layouts: 30.4 us -> 32.9 us
  transfers between devices with their start and end apart: 11 -> 14, of which waited for: 9 -> 11; matrix products, arithmetic and copies ran while one was open for 9% -> 8% of each run, Pallas kernels for 0% -> 0%
where the time goes in v1:
time: 1180 us; the launch traced here: 1170 us
  waiting for transfers between devices  776 us (66%)
  local copies, waits for them, and re-layouts  135 us (11%)
  matrix products  104 us (9%)
  blocking collectives  59.9 us (5%)
  other arithmetic  49.5 us (4%)
  starting transfers between devices  33.4 us (3%)
  between operations  14.9 us (1%)
    reduce_scatter x1, waiting for transfers between devices, on_device(): lax.psum_scatter(jnp.dot(grad_upward, w_mlp[:, 0, :], preferred_element_t...  144 us
    reduce_scatter x1, waiting for transfers between devices, holder_pass(): lax.psum_scatter(jnp.dot(mixed, w_out, preferred_element_type=jnp.float32...  143 us
    psum x1, waiting for transfers between devices, on_device(): lax.psum(qkv_local.astype(jnp.bfloat16), 'seq').astype(jnp.float32)  106 us
    ppermute x3, waiting for transfers between devices, make_the_outputs(): block_next = lax.ppermute(block_next, axis_id, in_order)  95.4 us
    all_gather x1, waiting for transfers between devices, on_device(): attended_all = lax.all_gather(grad_attended, 'mp', axis=0, tiled=True)  81.6 us
    all_gather x1, waiting for transfers between devices, holder_pass(): normed_all = lax.all_gather(normed_one, 'mp', axis=0, tiled=True)  80.2 us
    all_gather x1, waiting for transfers between devices, holder_pass(): normed_mid = lax.all_gather(normed_two, 'mp', axis=0, tiled=True)  71.2 us
    psum x1, blocking collectives, on_device(): lax.psum((attn_gain_part, mlp_gain_part, router_part), ('seq', 'mp'))  39.6 us
  transfers between devices with their start and end apart: 14, of which 11 were waited for; matrix products, arithmetic and copies ran while one was open for 8% of the time, Pallas kernels for 0%

profile of v1, /device:TPU:0, one launch (start us, length us, event | category | flops | bytes accessed | tf_op | source)
XLA Modules:
  0.0 1172.3 jit_solution(4361416221310719776)
XLA Ops:
  9.4 8.4 gather_fusion.1
  17.9 8.4 gather_fusion
  26.4 2.8 select_select_fusion
  29.2 20.3 %all_to_all.42 = bf16[8,2,1,32,1024]{4,3,1,2,0:T(8,128)(2,1)S(1)} all-to-all(bf16[8,2,1,32,1024]{4,3,1,2,0:T(8,128)(2,1)S(1)} %bitcast.192), channel_id=1, replica_groups=mesh['seq'=8,'mp'=4] {'seq'}, dimensions={0} | all-to-all | bytes 2097152 | tf_op jit(solution)/shard_map/all_to_all | solution.py:144
  53.2 80.2 %all-gather.4.cloned.1.call-done = bf16[2048,1024]{1,0:T(8,128)(2,1)} async-done(((bf16[512,1024]{1,0:T(8,128)(2,1)}), bf16[2048,1024]{1,0:T(8,128)(2,1)}) %all-gather.4.cloned.1.call-update) | async-done | bytes 4194320 | tf_op jit(solution)/shard_map/all_gather | solution.py:50
  133.4 5.6 fusion.25
  140.8 4.9 reshape.258
  145.7 3.9 copy.157
  149.6 4.4 reshape.257
  154.0 4.0 copy.156
  158.0 4.4 reshape.256
  162.4 4.0 copy.158
  166.3 3.9 fusion.71
  177.1 4.7 fusion.73
  181.9 143.1 %reduce-scatter.5.cloned.1.call-done = f32[512,1024]{1,0:T(8,128)} async-done(((f32[2048,1024]{1,0:T(8,128)}), f32[512,1024]{1,0:T(8,128)}) %reduce-scatter.5.cloned.1.call-update) | async-done | bytes 2097168 | tf_op jit(solution)/shard_map/reduce_scatter | solution.py:65
  328.7 10.4 fusion.69
  339.0 71.2 %all-gather.6.cloned.1.call-done = bf16[2048,1024]{1,0:T(8,128)(2,1)} async-done(((bf16[512,1024]{1,0:T(8,128)(2,1)}), bf16[2048,1024]{1,0:T(8,128)(2,1)}) %all-gather.6.cloned.1.call-update) | async-done | bytes 4194320 | tf_op jit(solution)/shard_map/all_gather | solution.py:75
  410.2 10.3 fusion.58
  420.6 3.4 copy-done.39
  424.0 7.3 convolution_convert_fusion
  431.3 4.2 all-to-all-start.2
  435.6 15.3 %all-to-all-done.2 = bf16[8,2,1,32,1024]{4,3,1,2,0:T(8,128)(2,1)} async-done(((bf16[8,2,1,32,1024]{4,3,1,2,0:T(8,128)(2,1)}), bf16[8,2,1,32,1024]{4,3,1,2,0:T(8,128)(2,1)}, u32[]{:S(2)}, u32[]{:S(2)}) %all-to-all-start.2) | async-done | bytes 1048608 | tf_op jit(solution)/shard_map/all_to_all | solution.py:151
  456.4 48.9 %collective-permute-done = bf16[512,1024]{1,0:T(8,128)(2,1)S(1)} collective-permute-done((bf16[512,1024]{1,0:T(8,128)(2,1)S(1)}, bf16[512,1024]{1,0:T(8,128)(2,1)S(1)}, u32[]{:S(2)}, u32[]{:S(2)}) %collective-permute-start) | collective-permute-done | bytes 1048608 | tf_op jit(solution)/shard_map/ppermute | solution.py:125
  506.3 19.9 %collective-permute-start.1 = (bf16[512,1024]{1,0:T(8,128)(2,1)S(1)}, bf16[512,1024]{1,0:T(8,128)(2,1)}, u32[]{:S(2)}, u32[]{:S(2)}) collective-permute-start(bf16[512,1024]{1,0:T(8,128)(2,1)S(1)} %collective-permute-done), channel_id=1, source_target_pairs={{0,1},{1,2},{2,3},{3,0},{4,5},{5,6},{6,7},{7,4},{8,9},{9,10},{10,1... | collective-permute-start | bytes 3145736 | tf_op jit(solution)/shard_map/ppermute | solution.py:125
  526.1 26.4 %collective-permute-done.1 = bf16[512,1024]{1,0:T(8,128)(2,1)} collective-permute-done((bf16[512,1024]{1,0:T(8,128)(2,1)S(1)}, bf16[512,1024]{1,0:T(8,128)(2,1)}, u32[]{:S(2)}, u32[]{:S(2)}) %collective-permute-start.1) | collective-permute-done | bytes 1048608 | tf_op jit(solution)/shard_map/ppermute | solution.py:125
  552.5 2.4 constant_dynamic-update-slice_fusion.5
  555.0 2.3 constant_dynamic-update-slice_fusion.4
  557.3 20.1 %collective-permute-done.2 = bf16[512,1024]{1,0:T(8,128)(2,1)} collective-permute-done((bf16[512,1024]{1,0:T(8,128)(2,1)}, bf16[512,1024]{1,0:T(8,128)(2,1)}, u32[]{:S(2)}, u32[]{:S(2)}) %collective-permute-start.2) | collective-permute-done | bytes 1048608 | tf_op jit(solution)/shard_map/ppermute | solution.py:125
  577.4 2.3 constant_dynamic-update-slice_fusion.3
  579.6 12.6 %fusion.10 = bf16[2048,1024]{1,0:T(8,128)(2,1)S(1)} fusion(f32[2048,1024]{1,0:T(8,128)} %copy-done.39, bf16[2048,1024]{1,0:T(8,128)(2,1)} %constant_dynamic-update-slice_fusion.3, bf16[1024,1,1024]{2,1,0:T(2,128)(2,1)S(1)} %copy-done.21), kind=kOutput, calls=%fused_computation.16 | convolution fusion | flops 4336910336 | bytes 18874368 | tf_op jit(solution)/shard_map/dot_general | solution.py:191
  594.2 6.9 fusion.57
  601.2 143.9 %reduce-scatter.9.cloned.1.call-done = f32[512,1024]{1,0:T(8,128)} async-done(((f32[2048,1024]{1,0:T(8,128)}), f32[512,1024]{1,0:T(8,128)}) %reduce-scatter.9.cloned.1.call-update) | async-done | bytes 2097168 | tf_op jit(solution)/shard_map/reduce_scatter | solution.py:201
  745.1 5.3 multiply_reduce_fusion.1
  752.3 81.6 %all-gather.8.cloned.1.call-done = bf16[2048,1024]{1,0:T(8,128)(2,1)} async-done(((bf16[512,1024]{1,0:T(8,128)(2,1)}), bf16[2048,1024]{1,0:T(8,128)(2,1)}) %all-gather.8.cloned.1.call-update) | async-done | bytes 4194320 | tf_op jit(solution)/shard_map/all_gather | solution.py:210
  833.8 4.5 convolution_convert_fusion.1
  838.3 4.8 reshape.259
  843.1 3.9 copy.168
  847.1 6.2 fusion.52
  853.3 5.6 multiply_reduce_fusion
  860.9 2.4 fusion.56
  865.1 4.0 copy.194
  869.1 4.3 reshape.255
  873.5 4.0 copy.192
  877.5 4.3 reshape.253
  881.8 4.0 copy.193
  885.8 4.3 reshape.254
  894.6 5.1 bitcast_convert_fusion
  899.9 8.2 convert_bitcast_fusion.2
  908.1 9.0 convert_bitcast_fusion.1
  917.1 2.5 pad_maximum_fusion
  921.1 2.1 convolution_convert_fusion.2
  924.5 4.5 fusion.44
  929.0 2.3 copy.163
  931.3 4.5 all-to-all-start.1
  935.8 39.3 %reduce-scatter.11.cloned.1.call-done = bf16[512,1024]{1,0:T(8,128)(2,1)} async-done(((bf16[2048,1024]{1,0:T(8,128)(2,1)}), bf16[512,1024]{1,0:T(8,128)(2,1)}) %reduce-scatter.11.cloned.1.call-update) | async-done | bytes 1048592 | tf_op jit(solution)/shard_map/reduce_scatter | solution.py:243
  977.2 3.2 fusion.35
  981.6 4.2 all-to-all-start.3
  986.8 2.8 bitcast_convert_fusion.2
  989.6 105.9 %all-reduce.4.cloned.1.call-done = (bf16[3,1024,256]{1,2,0:T(8,128)(2,1)}, bf16[1024,2,1024]{2,0,1:T(8,128)(2,1)}, bf16[256,1024]{1,0:T(8,128)(2,1)}) async-done(((bf16[3,1024,256]{1,2,0:T(8,128)(2,1)}, bf16[1024,2,1024]{2,0,1:T(8,128)(2,1)}, bf16[256,1024]{1,0:T(8,128)(2,1)}), (bf16[3,1024,256]{1,2,0:T(8,128)(2,1)}, bf16[1024,2,1024]{2,0,1:T(8,128)(2,1)}, ...) | async-done | bytes 6291472 | tf_op jit(solution)/shard_map/psum | solution.py:283
  1095.6 2.1 convert_element_type.200
  1097.7 3.1 copy.185
  1100.8 9.9 copy.186
  1110.7 39.6 %all-reduce = (f32[1024]{0:T(1024)}, f32[1024]{0:T(1024)}, f32[1024]{0:T(1024)}) all-reduce(f32[1024]{0:T(1024)S(1)} %get-tuple-element.51, f32[1024]{0:T(1024)S(1)} %get-tuple-element.49, f32[1024]{0:T(1024)S(1)} %bitcast.204), channel_id=1, replica_groups=mesh['seq'=8,'mp'=4] {'seq','mp'}, use_global_device_ids=true, to_apply=%region_13.15 | all-reduce | flops 3072 | bytes 24576 | tf_op jit(solution)/shard_map/psum | solution.py:287
  1152.1 13.1 %fusion.1 = (bf16[16,256,1024]{2,1,0:T(8,128)(2,1)}, bf16[16,256,1024]{2,1,0:T(8,128)(2,1)}) fusion(bf16[16,256,1024]{2,1,0:T(8,128)(2,1)} %param.13, f32[16,32,1024]{2,1,0:T(8,128)S(1)} %bitcast.185, pred[16,256]{1,0:T(8,128)(4,1)S(1)} %copy.149, f32[16,32,1024]{2,1,0:T(8,128)S(1)} %bitcast.184, bf16[16,256,1024]{2,1,0:T(8,128)(2,1)} %param.12), kind=kLoop, calls=%fused_computation.4 | loop fusion | flops 33554432 | bytes 37752832 | tf_op jit(solution)/shard_map/convert_element_type | solution.py:279
  (155 shorter events, 45.8 us)
Async XLA Ops:
  7.2 126.3 %copy-start = (bf16[3,1024,256]{2,1,0:T(8,128)(2,1)S(1)}, bf16[3,1024,256]{2,1,0:T(8,128)(2,1)}, u32[]{:S(2)}) copy-start(bf16[3,1024,256]{2,1,0:T(8,128)(2,1)} %param.19) | copy-start | bytes 4718596
  7.2 126.2 %all-gather.4.cloned.1.call-start = ((), (), s32[]{:S(2)}) async-start(), calls=%async_computation.8 | async-start | bytes 5242880 | tf_op jit(solution)/shard_map/all_gather | solution.py:50
  8.7 0.6 copy-start.26
  26.4 2.8 copy-start.33
  26.4 25.4 %copy-start.29 = (f32[1024]{0:T(1024)S(1)}, f32[1024]{0:T(1024)}, u32[]{:S(2)}) copy-start(f32[1024]{0:T(1024)} %param.16) | copy-start | bytes 12292
  49.5 1.0 copy-start.8
  50.5 88.6 %copy-start.31 = (f32[512]{0:T(512)}, f32[512]{0:T(512)S(1)}, u32[]{:S(2)}) copy-start(f32[512]{0:T(512)S(1)} %rsqrt.22) | copy-start | bytes 6148
  53.1 271.9 %reduce-scatter.5.cloned.1.call-start = ((), (), s32[]{:S(2)}) async-start(), calls=%async_computation.9 | async-start | bytes 10485760 | tf_op jit(solution)/shard_map/reduce_scatter | solution.py:65
  170.2 3.4 copy-start.1
  170.2 3.4 copy-start.13
  175.2 1.9 copy-start.23
  176.1 1.0 copy-start.11
  181.8 145.3 %copy-start.28 = (f32[1024]{0:T(1024)S(1)}, f32[1024]{0:T(1024)}, u32[]{:S(2)}) copy-start(f32[1024]{0:T(1024)} %param.17) | copy-start | bytes 12292
  181.8 228.4 %all-gather.6.cloned.1.call-start = ((), (), s32[]{:S(2)}) async-start(), calls=%async_computation.10 | async-start | bytes 5242880 | tf_op jit(solution)/shard_map/all_gather | solution.py:75
  325.0 2.2 copy-start.2
  328.6 272.6 %reduce-scatter.7.cloned.1.call-start = ((), (), s32[]{:S(2)}) async-start(), calls=%async_computation.11 | async-start | bytes 5242880 | tf_op jit(solution)/shard_map/reduce_scatter | solution.py:80
  410.2 13.7 %copy-start.20 = (bf16[1024,1,1024]{2,1,0:T(2,128)(2,1)S(1)}, bf16[1024,1,1024]{2,1,0:T(2,128)(2,1)}, u32[]{:S(2)}) copy-start(bf16[1024,1,1024]{2,1,0:T(2,128)(2,1)} %get-tuple-element.63) | copy-start | bytes 6291460
  420.6 3.4 copy-start.39
  431.3 19.7 %all-to-all-start.2 = ((bf16[8,2,1,32,1024]{4,3,1,2,0:T(8,128)(2,1)}), bf16[8,2,1,32,1024]{4,3,1,2,0:T(8,128)(2,1)}, u32[]{:S(2)}, u32[]{:S(2)}) async-start(bf16[8,2,1,32,1024]{4,3,1,2,0:T(8,128)(2,1)} %bitcast.190), calls=%async_computation.4 | async-start | bytes 2097152 | tf_op jit(solution)/shard_map/all_to_all | solution.py:151
  435.5 17.2 %copy-start.35 = (f32[1024]{0:T(1024)S(1)}, f32[1024]{0:T(1024)}, u32[]{:S(2)}) copy-start(f32[1024]{0:T(1024)} %param.18) | copy-start | bytes 12292
  435.5 309.5 %reduce-scatter.9.cloned.1.call-start = ((), (), s32[]{:S(2)}) async-start(), calls=%async_computation.12 | async-start | bytes 10485760 | tf_op jit(solution)/shard_map/reduce_scatter | solution.py:201
  452.7 1.7 copy-start.4
  454.4 2.0 copy-start.16
  456.4 48.9 %collective-permute-start = (bf16[512,1024]{1,0:T(8,128)(2,1)S(1)}, bf16[512,1024]{1,0:T(8,128)(2,1)S(1)}, u32[]{:S(2)}, u32[]{:S(2)}) collective-permute-start(bf16[512,1024]{1,0:T(8,128)(2,1)S(1)} %get-tuple-element.75), channel_id=1, source_target_pairs={{0,1},{1,2},{2,3},{3,0},{4,5},{5,6},{6,7},{7,4},{8,9},{9,10},{10,1... | collective-permute-start | bytes 3145736 | tf_op jit(solution)/shard_map/ppermute | solution.py:125
  505.3 1.0 copy-start.22
  506.3 46.3 %collective-permute-start.1 = (bf16[512,1024]{1,0:T(8,128)(2,1)S(1)}, bf16[512,1024]{1,0:T(8,128)(2,1)}, u32[]{:S(2)}, u32[]{:S(2)}) collective-permute-start(bf16[512,1024]{1,0:T(8,128)(2,1)S(1)} %collective-permute-done), channel_id=1, source_target_pairs={{0,1},{1,2},{2,3},{3,0},{4,5},{5,6},{6,7},{7,4},{8,9},{9,10},{10,1... | collective-permute-start | bytes 3145736 | tf_op jit(solution)/shard_map/ppermute | solution.py:125
  552.5 24.8 %collective-permute-start.2 = (bf16[512,1024]{1,0:T(8,128)(2,1)}, bf16[512,1024]{1,0:T(8,128)(2,1)}, u32[]{:S(2)}, u32[]{:S(2)}) collective-permute-start(bf16[512,1024]{1,0:T(8,128)(2,1)} %collective-permute-done.1), channel_id=1, source_target_pairs={{0,1},{1,2},{2,3},{3,0},{4,5},{5,6},{6,7},{7,4},{8,9},{9,10},{10,1... | collective-permute-start | bytes 3145736 | tf_op jit(solution)/shard_map/ppermute | solution.py:125
  552.5 27.1 %copy-start.21 = (bf16[1024,1,1024]{2,1,0:T(2,128)(2,1)S(1)}, bf16[1024,1,1024]{2,1,0:T(2,128)(2,1)}, u32[]{:S(2)}) copy-start(bf16[1024,1,1024]{2,1,0:T(2,128)(2,1)} %get-tuple-element.63) | copy-start | bytes 6291460
  579.6 14.6 %copy-start.19 = (bf16[1024,1,1024]{2,1,0:T(2,128)(2,1)S(1)}, bf16[1024,1,1024]{2,1,0:T(2,128)(2,1)}, u32[]{:S(2)}) copy-start(bf16[1024,1,1024]{2,1,0:T(2,128)(2,1)} %get-tuple-element.62) | copy-start | bytes 6291460
  592.3 1.9 copy-start.38
  601.1 232.7 %all-gather.8.cloned.1.call-start = ((), (), s32[]{:S(2)}) async-start(), calls=%async_computation.13 | async-start | bytes 5242880 | tf_op jit(solution)/shard_map/all_gather | solution.py:210
  745.1 5.3 copy-start.3
  745.1 5.3 copy-start.5
  745.1 5.3 copy-start.6
  752.2 222.9 %reduce-scatter.11.cloned.1.call-start = ((), (), s32[]{:S(2)}) async-start(), calls=%async_computation.14 | async-start | bytes 5242880 | tf_op jit(solution)/shard_map/reduce_scatter | solution.py:243
  847.0 6.2 copy-start.7
  847.0 6.2 copy-start.14
  847.0 11.8 %slice-start = ((s8[8388608]{0:T(1024)(128)(4,1)}), s8[4194304]{0:T(1024)(128)(4,1)S(1)}, s32[]{:S(2)}) async-start(s8[8388608]{0:T(1024)(128)(4,1)} %bitcast.177), calls=%async_computation.16 | async-start | bytes 8388608
  853.3 5.6 slice-start.1
  858.9 2.0 copy-start.18
  860.9 2.4 copy-start.10
  890.1 2.7 copy-start.15
  892.9 1.7 copy-start.24
  899.7 195.9 %all-reduce.4.cloned.1.call-start = ((), (), s32[]{:S(2)}) async-start(), calls=%async_computation.15 | async-start | bytes 12582912 | tf_op jit(solution)/shard_map/psum | solution.py:283
  899.9 8.2 copy-start.17
  917.1 2.5 copy-start.12
  917.1 4.0 copy-start.37
  921.1 2.1 copy-start.25
  921.1 3.3 copy-start.36
  929.0 46.1 %copy-start.30 = (f32[1024]{0:T(1024)S(1)}, f32[1024]{0:T(1024)}, u32[]{:S(2)}) copy-start(f32[1024]{0:T(1024)} %param.16) | copy-start | bytes 12292
  929.0 46.1 %copy-start.32 = (f32[512]{0:T(512)S(1)}, f32[512]{0:T(512)}, u32[]{:S(2)}) copy-start(f32[512]{0:T(512)} %copy-done.31) | copy-start | bytes 6148
  931.3 50.3 %all-to-all-start.1 = ((bf16[1,2,8,32,1024]{4,3,1,0,2:T(8,128)(2,1)}), bf16[1,2,8,32,1024]{4,3,1,0,2:T(8,128)(2,1)}, u32[]{:S(2)}, u32[]{:S(2)}) async-start(bf16[1,2,8,32,1024]{4,3,1,0,2:T(8,128)(2,1)} %copy.163), calls=%async_computation.3 | async-start | bytes 2097152 | tf_op jit(solution)/shard_map/all_to_all | solution.py:258
  977.2 8.6 copy-start.34
  977.2 8.7 copy-start.27
  981.6 168.7 %all-to-all-start.3 = ((bf16[1,2,8,32,1024]{4,3,1,0,2:T(8,128)(2,1)}), bf16[1,2,8,32,1024]{4,3,1,0,2:T(8,128)(2,1)}, u32[]{:S(2)}, u32[]{:S(2)}) async-start(bf16[1,2,8,32,1024]{4,3,1,0,2:T(8,128)(2,1)} %copy.182), calls=%async_computation.7 | async-start | bytes 2097152 | tf_op jit(solution)/shard_map/all_to_all | solution.py:265
  1150.2 1.9 copy-start.9
Sparse Core Ops, SparseCore 0:
  53.3 80.1 all-gather.3
  181.9 143.0 reduce-scatter.4
  328.7 81.4 all-gather.5
  431.4 100.3 reduce-scatter.6
  601.2 143.7 reduce-scatter.8
  752.3 81.4 all-gather.7
  899.8 75.2 reduce-scatter.10
  979.2 116.2 all-reduce.3
